TPU v7x, 32 devices: a whole 2x2x4 slice. The times are simulated.
32 devices in a mesh: sec: 2 (over y), blk: 16 (over z, x, core).
Axes of the slice: x: 2, y: 2, z: 4, core: 2. Of those that a mesh axis runs over, the one named last changes fastest.
Arguments:
- wave_speed: float32 [2, 125, 4096], P('sec', None, 'blk'), may hold values from 0.5 to 2
- inverse_mass: float32 [2, 125, 4096], P('sec', None, 'blk'), may hold values from 0.5 to 2
- source_field: float32 [2, 125, 4096], P('sec', None, 'blk'), may hold values from -4 to 4
- source_time: float32 [2, 12], P('sec'), may hold values from -4 to 4
- face_links: int32 [2, 3, 2048], P('sec', None, 'blk'), may hold values from 0 to 255, as said below
- coupling_links: int32 [5, 8192], P(None, 'blk'), may hold values from -1 to 255, as said below
Outputs:
- adjoint_now: float32 [2, 125, 4096], P('sec', None, 'blk')
- adjoint_before: float32 [2, 125, 4096], P('sec', None, 'blk')
Inputs may be any that keep to these rules, and one draw needn't show every extreme that they name: `face_links`: in each section record k of block b and record k of its peer name each other; the peer is b XOR 2^j for a bit j that depends on the section and k only, and equals b for unlinked records, which are the trailing ones. A block's records name distinct elements. A block has at most 16 records with one peer and exactly 16 with some peer. `coupling_links`: owner -1 marks unused points, which are the trailing points of a block. A box block has at most 4 points with one owner, and every box block has exactly 4 points with one common owner.
All inputs are finite; a program needn't handle non-finite values.
Results may differ from a plain program's by a relative error of at most 0.0001.
Values sent between devices are 32-bit elements; how exact they have to be, the bound alone decides.
No kernel may reach another device: no remote copies, remote signals or barrier semaphores. Data moves between devices by JAX's collectives and lax.ppermute only.
A program may use at most 64 MiB of HBM per device.

v0:
```python
import jax
import jax.numpy as jnp
import numpy as np
from jax import lax
from jax.sharding import PartitionSpec as P

CAPC = 4
STEPS = 12
DT_SQUARED = 0.05
PENALTY = 10.0


def partner_2(value, axis, stride):
    return lax.ppermute(value, axis, [(i, i ^ 1 << stride) for i in range(lax.axis_size(axis))])


def node_tables():
    abscissae = np.array([-1.0, -np.sqrt(3.0 / 7.0), 0.0, np.sqrt(3.0 / 7.0), 1.0])
    weights = np.array([0.1, 49.0 / 90.0, 32.0 / 45.0, 49.0 / 90.0, 0.1])
    legendre = (35.0 * abscissae**4 - 30.0 * abscissae**2 + 3.0) / 8.0
    derivative = np.zeros((5, 5))
    for i in range(5):
        for j in range(5):
            if i != j:
                derivative[i, j] = legendre[i] / (legendre[j] * (abscissae[i] - abscissae[j]))
    derivative[0, 0] = -2.5
    derivative[4, 4] = 2.5
    identity = np.eye(5)
    operator = np.concatenate(
        [
            np.kron(np.kron(derivative, identity), identity),
            np.kron(np.kron(identity, derivative), identity),
            np.kron(np.kron(identity, identity), derivative),
        ],
        axis=0,
    )
    weight_cube = weights[:, None, None] * weights[None, :, None] * weights[None, None, :]
    lattice = np.arange(125).reshape(5, 5, 5)
    face_nodes = np.stack(
        [
            lattice[0].ravel(),
            lattice[4].ravel(),
            lattice[:, 0].ravel(),
            lattice[:, 4].ravel(),
            lattice[:, :, 0].ravel(),
            lattice[:, :, 4].ravel(),
        ]
    )
    return (
        operator.astype(np.float32),
        weight_cube.reshape(125, 1).astype(np.float32),
        face_nodes.astype(np.int32),
    )


def stiffness(field_in, speed_sq, operator, weight_cube):
    columns = field_in.shape[-1]
    scaling = weight_cube * speed_sq
    grads = jnp.dot(
        operator, field_in, precision=lax.Precision.HIGHEST, preferred_element_type=jnp.float32
    )
    scaled = (grads.reshape(3, 125, columns) * scaling[None]).reshape(375, columns)
    return jnp.dot(
        operator.T, scaled, precision=lax.Precision.HIGHEST, preferred_element_type=jnp.float32
    )


def body(wave_speed, inverse_mass, source_field, source_time, face_links, coupling_links):
    operator_np, weight_np, faces_np = node_tables()
    operator = jnp.asarray(operator_np)
    weight_cube = jnp.asarray(weight_np)
    picker_np = np.zeros((150, 125), np.float32)
    for side_number in range(6):
        for node_number in range(25):
            picker_np[side_number * 25 + node_number, faces_np[side_number, node_number]] = 1.0
    picker = jnp.asarray(picker_np)
    spreader = jnp.asarray(picker_np.T.copy())
    speed_sq = wave_speed[0]
    inverse = inverse_mass[0]
    forcing = source_field[0]
    timing = source_time[0]
    element = face_links[0, 0]
    face_side = face_links[0, 1]
    face_peer = face_links[0, 2]
    blocks = lax.axis_size("blk")
    bit_count = blocks.bit_length() - 1
    myself = lax.axis_index("blk")
    is_box = lax.axis_index("sec") == 0
    records = element.shape[0]
    per_peer = records // 8
    ordinal = jnp.arange(records)
    linked = face_peer != myself
    side_mask = face_side[None, None, :] == jnp.arange(6, dtype=jnp.int32)[:, None, None]
    earlier = ordinal[None, :] < ordinal[:, None]
    face_slot = jnp.sum(
        ((face_peer[:, None] == face_peer[None, :]) & earlier).astype(jnp.int32), axis=1
    )
    offset_bits = jnp.bitwise_xor(face_peer, myself)
    bit_index = jnp.zeros((records,), jnp.int32)
    for bit_number in range(bit_count):
        bit_index = bit_index + bit_number * (offset_bits == 1 << bit_number).astype(jnp.int32)
    pair_column = jnp.where(linked, bit_index * per_peer + face_slot, 0)
    point_element = coupling_links[0]
    point_node = coupling_links[1]
    point_owner = coupling_links[2]
    target_element = coupling_links[3]
    target_node = coupling_links[4]
    in_use = point_owner >= 0
    owner_safe = jnp.maximum(point_owner, 0)
    point_ordinal = jnp.arange(point_owner.shape[0])
    point_earlier = point_ordinal[None, :] < point_ordinal[:, None]
    point_slot = jnp.sum(
        ((point_owner[:, None] == point_owner[None, :]) & point_earlier).astype(jnp.int32), axis=1
    )
    point_column = jnp.where(in_use, point_slot * blocks + owner_safe, 0)
    slot_total = CAPC * blocks
    outbound = jnp.zeros((3, slot_total), jnp.int32)
    outbound = outbound.at[0, point_column].add(jnp.where(in_use, target_element, 0))
    outbound = outbound.at[1, point_column].add(jnp.where(in_use, target_node, 0))
    outbound = outbound.at[2, point_column].add(in_use.astype(jnp.int32))
    inbound = lax.all_to_all(
        outbound.reshape(3, CAPC, blocks), "blk", split_axis=2, concat_axis=2, tiled=True
    ).reshape(3, slot_total)
    remote_element = inbound[0]
    remote_node = inbound[1]
    remote_flag = inbound[2].astype(jnp.float32)
    target_rows = jnp.concatenate([point_node, remote_node])
    target_cols = jnp.concatenate([point_element, remote_element])
    current = jnp.zeros(speed_sq.shape, jnp.float32)
    previous = jnp.zeros(speed_sq.shape, jnp.float32)
    for moment in range(STEPS):
        internal = stiffness(current, speed_sq, operator, weight_cube)
        stacked = jnp.dot(
            picker,
            internal[:, element],
            precision=lax.Precision.HIGHEST,
            preferred_element_type=jnp.float32,
        ).reshape(6, 25, records)
        payload = jnp.sum(jnp.where(side_mask, stacked, 0.0), axis=0)
        payload = jnp.where(linked[None, :], payload, 0.0)
        outgoing = (
            jnp.zeros((25, bit_count * per_peer), jnp.float32).at[:, pair_column].add(payload)
        )
        arrived = []
        for bit_number in range(bit_count):
            piece = outgoing[:, bit_number * per_peer : (bit_number + 1) * per_peer]
            arrived.append(partner_2(piece, "blk", bit_number))
        partner = jnp.concatenate(arrived, axis=1)[:, pair_column]
        partner = jnp.where(linked[None, :], partner, 0.0)
        masked = jnp.where(side_mask, partner[None], 0.0).reshape(150, records)
        assembled = internal.at[:, element].add(
            jnp.dot(
                spreader,
                masked,
                precision=lax.Precision.HIGHEST,
                preferred_element_type=jnp.float32,
            )
        )
        velocity = current - previous
        traction = assembled[point_node, point_element]
        box_send = (
            jnp.zeros((slot_total,), jnp.float32)
            .at[point_column]
            .add(jnp.where(in_use, traction, 0.0))
        )
        global_send = velocity[remote_node, remote_element] * remote_flag
        dispatch = jnp.where(is_box, box_send, global_send).reshape(CAPC, blocks)
        crossed = partner_2(dispatch, "sec", 0)
        received = lax.all_to_all(crossed, "blk", split_axis=1, concat_axis=1, tiled=True)
        received = received.reshape(slot_total)
        remote_velocity = received[point_column]
        box_terms = jnp.where(
            in_use, PENALTY * (remote_velocity - velocity[point_node, point_element]), 0.0
        )
        values = jnp.concatenate(
            [jnp.where(is_box, box_terms, 0.0), jnp.where(is_box, 0.0, received * remote_flag)]
        )
        driving = timing[moment] * forcing - assembled
        driving = driving.at[target_rows, target_cols].add(values)
        advanced = 2.0 * current - previous + DT_SQUARED * inverse * driving
        previous = current
        current = advanced
    return (current[None], previous[None])


def solution(mesh):
    in_specs = (
        P("sec", None, "blk"),
        P("sec", None, "blk"),
        P("sec", None, "blk"),
        P("sec", None),
        P("sec", None, "blk"),
        P(None, "blk"),
    )
    out_specs = (P("sec", None, "blk"), P("sec", None, "blk"))
    return jax.shard_map(body, mesh=mesh, in_specs=in_specs, out_specs=out_specs, check_vma=False)
```

profile of v0, /device:TPU:0, one launch (start us, length us, event | category | flops | bytes accessed | tf_op | source)
XLA Modules:
  0.0 1408.7 jit_solution(6198110718570769417)
XLA Ops:
  24.5 22.8 %scatter_fusion.1 = s32[3,64]{1,0:T(4,128)S(1)} fusion(s32[3,64]{1,0:T(4,128)S(1)} %broadcast_in_dim.578, s32[512]{0:T(512)S(1)} %bitcast.1117, s32[512]{0:T(512)S(1)} %get-tuple-element.946), kind=kCustom, calls=%fused_computation.62 | custom fusion | flops 512 | bytes 10240 | tf_op jit(solution)/shard_map/scatter-add | solution.py:118
  47.3 22.8 %scatter_fusion.2 = s32[3,64]{1,0:T(4,128)S(1)} fusion(s32[3,64]{1,0:T(4,128)S(1)} %scatter_fusion.1, s32[512]{0:T(512)S(1)} %bitcast.1116, s32[512]{0:T(512)S(1)} %get-tuple-element.945), kind=kCustom, calls=%fused_computation.63 | custom fusion | flops 512 | bytes 10240 | tf_op jit(solution)/shard_map/scatter-add | solution.py:119
  70.0 22.8 %scatter_fusion.3 = s32[3,64]{1,0:T(4,128)S(1)} fusion(s32[3,64]{1,0:T(4,128)S(1)} %scatter_fusion.2, s32[512]{0:T(512)S(1)} %bitcast.1115, s32[512]{0:T(512)S(1)} %convert_element_type.31), kind=kCustom, calls=%fused_computation.64 | custom fusion | flops 512 | bytes 10240 | tf_op jit(solution)/shard_map/scatter-add | solution.py:120
  112.4 6.2 all-to-all-start.1
  118.6 6.3 all-to-all-done.1
  128.0 40.1 %fusion.83 = (f32[512]{0:T(512)S(1)}, pred[512]{0:T(512)(128)(4,1)S(1)}, pred[512]{0:T(512)(128)(4,1)S(1)}, pred[512]{0:T(512)(128)(4,1)S(1)}, pred[512]{0:T(512...) fusion(pred[512]{0:T(512)(128)(4,1)S(1)} %get-tuple-element.99,, ...), kind=kLoop, calls=%fused_computation.341 | loop fusion | flops 66560 | bytes 39169 | tf_op jit(solution)/shard_map/jit(_where)/select_n | solution.py:176
  168.1 30.1 %scatter_fusion.4 = f32[125,256]{1,0:T(8,128)S(1)} fusion(f32[125,256]{1,0:T(8,128)S(1)} %copy.421, s32[576]{0:T(1024)S(1)} %fusion.42, f32[576]{0:T(1024)S(1)} %pad_maximum_fusion.12), kind=kCustom, calls=%fused_computation.66 | custom fusion | flops 576 | bytes 11520 | tf_op jit(solution)/shard_map/scatter-add | solution.py:179
  238.2 40.1 %fusion.80 = f32[512]{0:T(512)S(1)} fusion(pred[512]{0:T(512)(128)(4,1)S(1)} %get-tuple-element.99, f32[512]{0:T(512)S(1)} %gather_fusion.9, pred[512]{0:T(512)(128)(4,1)S(1)} %get-tuple-element.97, pred[512]{0:T(512)(128)(4,1)S(1)} %get-tuple-element.96, pred[512]{0:T(512)(128)(4,1)S(1)} %get-tuple-element.95, pred[512]{0:T(512)(128)(4,1)S(1)} %get-tuple-element.94, ...), kind=kLoop, calls=%fused_computation.337 | loop fusion | flops 34304 | bytes 37121 | tf_op jit(solution)/shard_map/jit(_where)/select_n | solution.py:176
  278.3 30.1 %scatter_fusion.6 = f32[125,256]{1,0:T(8,128)S(1)} fusion(f32[125,256]{1,0:T(8,128)S(1)} %copy.429, s32[576]{0:T(1024)S(1)} %fusion.42, f32[576]{0:T(1024)S(1)} %pad_maximum_fusion.13), kind=kCustom, calls=%fused_computation.70 | custom fusion | flops 576 | bytes 11520 | tf_op jit(solution)/shard_map/scatter-add | solution.py:179
  339.2 5.6 all-to-all-done.3
  347.8 40.0 %fusion.77 = f32[512]{0:T(512)S(1)} fusion(pred[512]{0:T(512)(128)(4,1)S(1)} %get-tuple-element.99, f32[512]{0:T(512)S(1)} %gather_fusion.14, pred[512]{0:T(512)(128)(4,1)S(1)} %get-tuple-element.97, pred[512]{0:T(512)(128)(4,1)S(1)} %get-tuple-element.96, pred[512]{0:T(512)(128)(4,1)S(1)} %get-tuple-element.95, pred[512]{0:T(512)(128)(4,1)S(1)} %get-tuple-element.94, ...), kind=kLoop, calls=%fused_computation.333 | loop fusion | flops 34304 | bytes 37121 | tf_op jit(solution)/shard_map/jit(_where)/select_n | solution.py:176
  387.9 30.1 %scatter_fusion.8 = f32[125,256]{1,0:T(8,128)S(1)} fusion(f32[125,256]{1,0:T(8,128)S(1)} %copy.437, s32[576]{0:T(1024)S(1)} %fusion.42, f32[576]{0:T(1024)S(1)} %pad_maximum_fusion.14), kind=kCustom, calls=%fused_computation.74 | custom fusion | flops 576 | bytes 11520 | tf_op jit(solution)/shard_map/scatter-add | solution.py:179
  458.2 40.1 %fusion.74 = f32[512]{0:T(512)S(1)} fusion(pred[512]{0:T(512)(128)(4,1)S(1)} %get-tuple-element.99, f32[512]{0:T(512)S(1)} %gather_fusion.19, pred[512]{0:T(512)(128)(4,1)S(1)} %get-tuple-element.97, pred[512]{0:T(512)(128)(4,1)S(1)} %get-tuple-element.96, pred[512]{0:T(512)(128)(4,1)S(1)} %get-tuple-element.95, pred[512]{0:T(512)(128)(4,1)S(1)} %get-tuple-element.94, ...), kind=kLoop, calls=%fused_computation.329 | loop fusion | flops 34304 | bytes 37121 | tf_op jit(solution)/shard_map/jit(_where)/select_n | solution.py:176
  498.3 30.1 %scatter_fusion.10 = f32[125,256]{1,0:T(8,128)S(1)} fusion(f32[125,256]{1,0:T(8,128)S(1)} %copy.445, s32[576]{0:T(1024)S(1)} %fusion.42, f32[576]{0:T(1024)S(1)} %pad_maximum_fusion.15), kind=kCustom, calls=%fused_computation.78 | custom fusion | flops 576 | bytes 11520 | tf_op jit(solution)/shard_map/scatter-add | solution.py:179
  558.7 5.6 all-to-all-done.5
  567.4 39.9 %fusion.71 = f32[512]{0:T(512)S(1)} fusion(pred[512]{0:T(512)(128)(4,1)S(1)} %get-tuple-element.99, f32[512]{0:T(512)S(1)} %gather_fusion.24, pred[512]{0:T(512)(128)(4,1)S(1)} %get-tuple-element.97, pred[512]{0:T(512)(128)(4,1)S(1)} %get-tuple-element.96, pred[512]{0:T(512)(128)(4,1)S(1)} %get-tuple-element.95, pred[512]{0:T(512)(128)(4,1)S(1)} %get-tuple-element.94, ...), kind=kLoop, calls=%fused_computation.325 | loop fusion | flops 34304 | bytes 37121 | tf_op jit(solution)/shard_map/jit(_where)/select_n | solution.py:176
  607.4 30.1 %scatter_fusion.12 = f32[125,256]{1,0:T(8,128)S(1)} fusion(f32[125,256]{1,0:T(8,128)S(1)} %copy.453, s32[576]{0:T(1024)S(1)} %fusion.42, f32[576]{0:T(1024)S(1)} %pad_maximum_fusion.16), kind=kCustom, calls=%fused_computation.82 | custom fusion | flops 576 | bytes 11520 | tf_op jit(solution)/shard_map/scatter-add | solution.py:179
  677.7 40.0 %fusion.68 = f32[512]{0:T(512)S(1)} fusion(pred[512]{0:T(512)(128)(4,1)S(1)} %get-tuple-element.99, f32[512]{0:T(512)S(1)} %gather_fusion.29, pred[512]{0:T(512)(128)(4,1)S(1)} %get-tuple-element.97, pred[512]{0:T(512)(128)(4,1)S(1)} %get-tuple-element.96, pred[512]{0:T(512)(128)(4,1)S(1)} %get-tuple-element.95, pred[512]{0:T(512)(128)(4,1)S(1)} %get-tuple-element.94, ...), kind=kLoop, calls=%fused_computation.321 | loop fusion | flops 34304 | bytes 37121 | tf_op jit(solution)/shard_map/jit(_where)/select_n | solution.py:176
  717.8 30.1 %scatter_fusion.14 = f32[125,256]{1,0:T(8,128)S(1)} fusion(f32[125,256]{1,0:T(8,128)S(1)} %copy.461, s32[576]{0:T(1024)S(1)} %fusion.42, f32[576]{0:T(1024)S(1)} %pad_maximum_fusion.17), kind=kCustom, calls=%fused_computation.86 | custom fusion | flops 576 | bytes 11520 | tf_op jit(solution)/shard_map/scatter-add | solution.py:179
  787.3 40.0 %fusion.65 = f32[512]{0:T(512)S(1)} fusion(pred[512]{0:T(512)(128)(4,1)S(1)} %get-tuple-element.99, f32[512]{0:T(512)S(1)} %gather_fusion.34, pred[512]{0:T(512)(128)(4,1)S(1)} %get-tuple-element.97, pred[512]{0:T(512)(128)(4,1)S(1)} %get-tuple-element.96, pred[512]{0:T(512)(128)(4,1)S(1)} %get-tuple-element.95, pred[512]{0:T(512)(128)(4,1)S(1)} %get-tuple-element.94, ...), kind=kLoop, calls=%fused_computation.317 | loop fusion | flops 34304 | bytes 37121 | tf_op jit(solution)/shard_map/jit(_where)/select_n | solution.py:176
  827.3 30.1 %scatter_fusion.16 = f32[125,256]{1,0:T(8,128)S(1)} fusion(f32[125,256]{1,0:T(8,128)S(1)} %copy.469, s32[576]{0:T(1024)S(1)} %fusion.42, f32[576]{0:T(1024)S(1)} %pad_maximum_fusion.18), kind=kCustom, calls=%fused_computation.90 | custom fusion | flops 576 | bytes 11520 | tf_op jit(solution)/shard_map/scatter-add | solution.py:179
  897.5 40.0 %fusion.62 = f32[512]{0:T(512)S(1)} fusion(pred[512]{0:T(512)(128)(4,1)S(1)} %get-tuple-element.99, f32[512]{0:T(512)S(1)} %gather_fusion.39, pred[512]{0:T(512)(128)(4,1)S(1)} %get-tuple-element.97, pred[512]{0:T(512)(128)(4,1)S(1)} %get-tuple-element.96, pred[512]{0:T(512)(128)(4,1)S(1)} %get-tuple-element.95, pred[512]{0:T(512)(128)(4,1)S(1)} %get-tuple-element.94, ...), kind=kLoop, calls=%fused_computation.313 | loop fusion | flops 34304 | bytes 37121 | tf_op jit(solution)/shard_map/jit(_where)/select_n | solution.py:176
  937.5 30.1 %scatter_fusion.18 = f32[125,256]{1,0:T(8,128)S(1)} fusion(f32[125,256]{1,0:T(8,128)S(1)} %copy.477, s32[576]{0:T(1024)S(1)} %fusion.42, f32[576]{0:T(1024)S(1)} %pad_maximum_fusion.19), kind=kCustom, calls=%fused_computation.94 | custom fusion | flops 576 | bytes 11520 | tf_op jit(solution)/shard_map/scatter-add | solution.py:179
  1006.8 40.0 %fusion.59 = f32[512]{0:T(512)S(1)} fusion(pred[512]{0:T(512)(128)(4,1)S(1)} %get-tuple-element.99, f32[512]{0:T(512)S(1)} %gather_fusion.44, pred[512]{0:T(512)(128)(4,1)S(1)} %get-tuple-element.97, pred[512]{0:T(512)(128)(4,1)S(1)} %get-tuple-element.96, pred[512]{0:T(512)(128)(4,1)S(1)} %get-tuple-element.95, pred[512]{0:T(512)(128)(4,1)S(1)} %get-tuple-element.94, ...), kind=kLoop, calls=%fused_computation.309 | loop fusion | flops 34304 | bytes 37121 | tf_op jit(solution)/shard_map/jit(_where)/select_n | solution.py:176
  1046.9 30.1 %scatter_fusion.20 = f32[125,256]{1,0:T(8,128)S(1)} fusion(f32[125,256]{1,0:T(8,128)S(1)} %copy.485, s32[576]{0:T(1024)S(1)} %fusion.42, f32[576]{0:T(1024)S(1)} %pad_maximum_fusion.20), kind=kCustom, calls=%fused_computation.98 | custom fusion | flops 576 | bytes 11520 | tf_op jit(solution)/shard_map/scatter-add | solution.py:179
  1117.2 40.0 %fusion.56 = f32[512]{0:T(512)S(1)} fusion(pred[512]{0:T(512)(128)(4,1)S(1)} %get-tuple-element.99, f32[512]{0:T(512)S(1)} %gather_fusion.49, pred[512]{0:T(512)(128)(4,1)S(1)} %get-tuple-element.97, pred[512]{0:T(512)(128)(4,1)S(1)} %get-tuple-element.96, pred[512]{0:T(512)(128)(4,1)S(1)} %get-tuple-element.95, pred[512]{0:T(512)(128)(4,1)S(1)} %get-tuple-element.94, ...), kind=kLoop, calls=%fused_computation.305 | loop fusion | flops 34304 | bytes 37121 | tf_op jit(solution)/shard_map/jit(_where)/select_n | solution.py:176
  1157.2 30.1 %scatter_fusion.22 = f32[125,256]{1,0:T(8,128)S(1)} fusion(f32[125,256]{1,0:T(8,128)S(1)} %copy.493, s32[576]{0:T(1024)S(1)} %fusion.42, f32[576]{0:T(1024)S(1)} %pad_maximum_fusion.21), kind=kCustom, calls=%fused_computation.102 | custom fusion | flops 576 | bytes 11520 | tf_op jit(solution)/shard_map/scatter-add | solution.py:179
  1217.7 5.6 all-to-all-done.11
  1226.4 39.9 %fusion.53 = f32[512]{0:T(512)S(1)} fusion(pred[512]{0:T(512)(128)(4,1)S(1)} %get-tuple-element.99, f32[512]{0:T(512)S(1)} %gather_fusion.54, pred[512]{0:T(512)(128)(4,1)S(1)} %get-tuple-element.97, pred[512]{0:T(512)(128)(4,1)S(1)} %get-tuple-element.96, pred[512]{0:T(512)(128)(4,1)S(1)} %get-tuple-element.95, pred[512]{0:T(512)(128)(4,1)S(1)} %get-tuple-element.94, ...), kind=kLoop, calls=%fused_computation.301 | loop fusion | flops 34304 | bytes 37121 | tf_op jit(solution)/shard_map/jit(_where)/select_n | solution.py:176
  1266.2 30.1 %scatter_fusion.24 = f32[125,256]{1,0:T(8,128)S(1)} fusion(f32[125,256]{1,0:T(8,128)S(1)} %copy.501, s32[576]{0:T(1024)S(1)} %fusion.42, f32[576]{0:T(1024)S(1)} %pad_maximum_fusion.22), kind=kCustom, calls=%fused_computation.106 | custom fusion | flops 576 | bytes 11520 | tf_op jit(solution)/shard_map/scatter-add | solution.py:179
  1337.4 39.9 %fusion.50 = f32[512]{0:T(512)S(1)} fusion(pred[512]{0:T(512)(128)(4,1)S(1)} %get-tuple-element.99, f32[512]{0:T(512)S(1)} %gather_fusion.59, pred[512]{0:T(512)(128)(4,1)S(1)} %get-tuple-element.97, pred[512]{0:T(512)(128)(4,1)S(1)} %get-tuple-element.96, pred[512]{0:T(512)(128)(4,1)S(1)} %get-tuple-element.95, pred[512]{0:T(512)(128)(4,1)S(1)} %get-tuple-element.94, ...), kind=kLoop, calls=%fused_computation.297 | loop fusion | flops 34304 | bytes 37121 | tf_op jit(solution)/shard_map/jit(_where)/select_n | solution.py:176
  1377.3 30.1 %scatter_fusion.26 = f32[125,256]{1,0:T(8,128)S(1)} fusion(f32[125,256]{1,0:T(8,128)S(1)} %copy.509, s32[576]{0:T(1024)S(1)} %fusion.42, f32[576]{0:T(1024)S(1)} %pad_maximum_fusion.23), kind=kCustom, calls=%fused_computation.110 | custom fusion | flops 576 | bytes 11520 | tf_op jit(solution)/shard_map/scatter-add | solution.py:179
  (638 shorter events, 465.8 us)
Async XLA Ops:
  7.8 7.6 collective-permute-start
  8.3 7.1 collective-permute-start.3
  93.6 13.0 all-to-all-start
  112.4 12.6 all-to-all-start.1
  217.5 6.0 collective-permute-start.9
  224.2 11.0 all-to-all-start.2
  312.7 4.7 collective-permute-start.13
  328.1 5.0 collective-permute-start.14
  333.8 11.0 all-to-all-start.3
  421.9 4.6 collective-permute-start.18
  437.2 6.0 collective-permute-start.19
  444.0 11.2 all-to-all-start.4
  547.6 5.0 collective-permute-start.24
  553.3 11.0 all-to-all-start.5
  656.9 6.0 collective-permute-start.29
  663.7 11.0 all-to-all-start.6
  767.1 5.0 collective-permute-start.34
  772.8 11.4 all-to-all-start.7
  876.7 6.1 collective-permute-start.39
  883.4 11.0 all-to-all-start.8
  971.6 4.7 collective-permute-start.43
  987.0 5.0 collective-permute-start.44
  992.7 11.0 all-to-all-start.9
  1080.8 4.7 collective-permute-start.48
  1096.2 6.0 collective-permute-start.49
  1102.9 11.2 all-to-all-start.10
  1191.2 4.7 collective-permute-start.53
  1206.6 5.0 collective-permute-start.54
  1212.3 11.0 all-to-all-start.11
  1300.5 4.7 collective-permute-start.58
  1315.8 6.8 collective-permute-start.59
  1323.4 11.0 all-to-all-start.12
  (50 other events, 222.3 us)
where the time goes:
time: 1420 us; the launch traced here: 1410 us
  other arithmetic  1000 us (70%)
  local copies, waits for them, and re-layouts  181 us (13%)
  starting transfers between devices  102 us (7%)
  waiting for transfers between devices  94.7 us (7%)
  matrix products  23.8 us (2%)
    select_n x12, other arithmetic, body(): jnp.where(is_box, box_terms, 0.0)  480 us
    scatter-add x12, other arithmetic, body(): driving = driving.at[target_rows, target_cols].add(values)  362 us
    all_to_all x12, waiting for transfers between devices, body(): lax.all_to_all(crossed, 'blk', split_axis=1, concat_axis=1, tiled=True)  67.6 us
    all_to_all x12, starting transfers between devices, body(): lax.all_to_all(crossed, 'blk', split_axis=1, concat_axis=1, tiled=True)  58.6 us
    gather x12, local copies, waits for them, and re-layouts, body(): velocity[point_node, point_element]  54.2 us
    scatter-add x12, other arithmetic, body(): box_send = jnp.zeros((slot_total,), jnp.float32).at[point_column].add(jnp...  49 us
    gather x12, local copies, waits for them, and re-layouts, body(): traction = assembled[point_node, point_element]  45 us
    ppermute x60, starting transfers between devices, partner_2(): lax.ppermute(value, axis, [(i, i ^ 1 << stride) for i in range(lax.axis_s...  40.2 us
  transfers between devices with their start and end apart: 73, of which 37 were waited for; matrix products, arithmetic and copies ran while one was open for 6% of the time, Pallas kernels for 0%

commit v1 on v0

--- a/solution.py
+++ b/solution.py
@@ -166,7 +166,12 @@
         global_send = velocity[remote_node, remote_element] * remote_flag
         dispatch = jnp.where(is_box, box_send, global_send).reshape(CAPC, blocks)
         crossed = partner_2(dispatch, "sec", 0)
-        received = lax.all_to_all(crossed, "blk", split_axis=1, concat_axis=1, tiled=True)
+        received = jnp.concatenate(
+            lax.all_to_all(
+                jnp.stack(jnp.split(crossed, lax.axis_size("blk"), axis=1)), "blk", 0, 0
+            ),
+            axis=1,
+        )
         received = received.reshape(slot_total)
         remote_velocity = received[point_column]
         box_terms = jnp.where(

time: 1420 us -> 1520 us (1.070)
  local copies, waits for them, and re-layouts: 181 us -> 277 us
    unnamed x23 -> x203, local copies, waits for them, and re-layouts: 5.08 us -> 97.2 us
  transfers between devices with their start and end apart: 73 -> 73, of which waited for: 37 -> 37; matrix products, arithmetic and copies ran while one was open for 6% -> 5% of each run, Pallas kernels for 0% -> 0%
where the time goes in v1:
time: 1520 us; the launch traced here: 1510 us
  other arithmetic  1000 us (66%)
  local copies, waits for them, and re-layouts  277 us (18%)
  starting transfers between devices  104 us (7%)
  waiting for transfers between devices  95 us (6%)
  matrix products  23.8 us (2%)
    select_n x12, other arithmetic, body(): jnp.where(is_box, box_terms, 0.0)  480 us
    scatter-add x12, other arithmetic, body(): driving = driving.at[target_rows, target_cols].add(values)  362 us
    unnamed x203, local copies, waits for them, and re-layouts  97.2 us
    all_to_all x12, waiting for transfers between devices, body(): lax.all_to_all(jnp.stack(jnp.split(crossed, lax.axis_size('blk'), axis=1)...  67.9 us
    all_to_all x12, starting transfers between devices, body(): lax.all_to_all(jnp.stack(jnp.split(crossed, lax.axis_size('blk'), axis=1)...  60.5 us
    gather x12, local copies, waits for them, and re-layouts, body(): velocity[point_node, point_element]  54.2 us
    scatter-add x12, other arithmetic, body(): box_send = jnp.zeros((slot_total,), jnp.float32).at[point_column].add(jnp...  49 us
    gather x12, local copies, waits for them, and re-layouts, body(): traction = assembled[point_node, point_element]  45 us
  transfers between devices with their start and end apart: 73, of which 37 were waited for; matrix products, arithmetic and copies ran while one was open for 5% of the time, Pallas kernels for 0%

profile of v1, /device:TPU:0, one launch (start us, length us, event | category | flops | bytes accessed | tf_op | source)
XLA Modules:
  0.0 1505.4 jit_solution(3803390146830561335)
XLA Ops:
  24.5 22.8 %scatter_fusion.1 = s32[3,64]{1,0:T(4,128)S(1)} fusion(s32[3,64]{1,0:T(4,128)S(1)} %broadcast_in_dim.578, s32[512]{0:T(512)S(1)} %bitcast.1501, s32[512]{0:T(512)S(1)} %get-tuple-element.1140), kind=kCustom, calls=%fused_computation.62 | custom fusion | flops 512 | bytes 10240 | tf_op jit(solution)/shard_map/scatter-add | solution.py:118
  47.3 22.8 %scatter_fusion.2 = s32[3,64]{1,0:T(4,128)S(1)} fusion(s32[3,64]{1,0:T(4,128)S(1)} %scatter_fusion.1, s32[512]{0:T(512)S(1)} %bitcast.1500, s32[512]{0:T(512)S(1)} %get-tuple-element.1139), kind=kCustom, calls=%fused_computation.63 | custom fusion | flops 512 | bytes 10240 | tf_op jit(solution)/shard_map/scatter-add | solution.py:119
  70.0 22.8 %scatter_fusion.3 = s32[3,64]{1,0:T(4,128)S(1)} fusion(s32[3,64]{1,0:T(4,128)S(1)} %scatter_fusion.2, s32[512]{0:T(512)S(1)} %bitcast.1499, s32[512]{0:T(512)S(1)} %convert_element_type.31), kind=kCustom, calls=%fused_computation.64 | custom fusion | flops 512 | bytes 10240 | tf_op jit(solution)/shard_map/scatter-add | solution.py:120
  120.4 6.2 all-to-all-start.1
  126.6 6.3 all-to-all-done.1
  135.9 40.1 %fusion.83 = (f32[512]{0:T(512)S(1)}, pred[512]{0:T(512)(128)(4,1)S(1)}, pred[512]{0:T(512)(128)(4,1)S(1)}, pred[512]{0:T(512)(128)(4,1)S(1)}, pred[512]{0:T(512...) fusion(pred[512]{0:T(512)(128)(4,1)S(1)} %get-tuple-element.293, ...), kind=kLoop, calls=%fused_computation.533 | loop fusion | flops 66560 | bytes 39169 | tf_op jit(solution)/shard_map/jit(_where)/select_n | solution.py:181
  176.0 30.1 %scatter_fusion.4 = f32[125,256]{1,0:T(8,128)S(1)} fusion(f32[125,256]{1,0:T(8,128)S(1)} %copy.907, s32[576]{0:T(1024)S(1)} %fusion.42, f32[576]{0:T(1024)S(1)} %pad_maximum_fusion.12), kind=kCustom, calls=%fused_computation.66 | custom fusion | flops 576 | bytes 11520 | tf_op jit(solution)/shard_map/scatter-add | solution.py:184
  254.4 40.1 %fusion.80 = f32[512]{0:T(512)S(1)} fusion(pred[512]{0:T(512)(128)(4,1)S(1)} %get-tuple-element.293, f32[512]{0:T(512)S(1)} %gather_fusion.9, pred[512]{0:T(512)(128)(4,1)S(1)} %get-tuple-element.291, pred[512]{0:T(512)(128)(4,1)S(1)} %get-tuple-element.290, pred[512]{0:T(512)(128)(4,1)S(1)} %get-tuple-element.289, ...), kind=kLoop, calls=%fused_computation.529 | loop fusion | flops 34304 | bytes 37121 | tf_op jit(solution)/shard_map/jit(_where)/select_n | solution.py:181
  294.5 30.1 %scatter_fusion.6 = f32[125,256]{1,0:T(8,128)S(1)} fusion(f32[125,256]{1,0:T(8,128)S(1)} %copy.914, s32[576]{0:T(1024)S(1)} %fusion.42, f32[576]{0:T(1024)S(1)} %pad_maximum_fusion.13), kind=kCustom, calls=%fused_computation.70 | custom fusion | flops 576 | bytes 11520 | tf_op jit(solution)/shard_map/scatter-add | solution.py:184
  363.4 5.7 all-to-all-done.3
  372.1 40.0 %fusion.77 = f32[512]{0:T(512)S(1)} fusion(pred[512]{0:T(512)(128)(4,1)S(1)} %get-tuple-element.293, f32[512]{0:T(512)S(1)} %gather_fusion.14, pred[512]{0:T(512)(128)(4,1)S(1)} %get-tuple-element.291, pred[512]{0:T(512)(128)(4,1)S(1)} %get-tuple-element.290, pred[512]{0:T(512)(128)(4,1)S(1)} %get-tuple-element.289, ...), kind=kLoop, calls=%fused_computation.525 | loop fusion | flops 34304 | bytes 37121 | tf_op jit(solution)/shard_map/jit(_where)/select_n | solution.py:181
  412.1 30.1 %scatter_fusion.8 = f32[125,256]{1,0:T(8,128)S(1)} fusion(f32[125,256]{1,0:T(8,128)S(1)} %copy.921, s32[576]{0:T(1024)S(1)} %fusion.42, f32[576]{0:T(1024)S(1)} %pad_maximum_fusion.14), kind=kCustom, calls=%fused_computation.74 | custom fusion | flops 576 | bytes 11520 | tf_op jit(solution)/shard_map/scatter-add | solution.py:184
  490.4 40.1 %fusion.74 = f32[512]{0:T(512)S(1)} fusion(pred[512]{0:T(512)(128)(4,1)S(1)} %get-tuple-element.293, f32[512]{0:T(512)S(1)} %gather_fusion.19, pred[512]{0:T(512)(128)(4,1)S(1)} %get-tuple-element.291, pred[512]{0:T(512)(128)(4,1)S(1)} %get-tuple-element.290, pred[512]{0:T(512)(128)(4,1)S(1)} %get-tuple-element.289, ...), kind=kLoop, calls=%fused_computation.521 | loop fusion | flops 34304 | bytes 37121 | tf_op jit(solution)/shard_map/jit(_where)/select_n | solution.py:181
  530.5 30.1 %scatter_fusion.10 = f32[125,256]{1,0:T(8,128)S(1)} fusion(f32[125,256]{1,0:T(8,128)S(1)} %copy.928, s32[576]{0:T(1024)S(1)} %fusion.42, f32[576]{0:T(1024)S(1)} %pad_maximum_fusion.15), kind=kCustom, calls=%fused_computation.78 | custom fusion | flops 576 | bytes 11520 | tf_op jit(solution)/shard_map/scatter-add | solution.py:184
  599.1 5.7 all-to-all-done.5
  607.8 39.9 %fusion.71 = f32[512]{0:T(512)S(1)} fusion(pred[512]{0:T(512)(128)(4,1)S(1)} %get-tuple-element.293, f32[512]{0:T(512)S(1)} %gather_fusion.24, pred[512]{0:T(512)(128)(4,1)S(1)} %get-tuple-element.291, pred[512]{0:T(512)(128)(4,1)S(1)} %get-tuple-element.290, pred[512]{0:T(512)(128)(4,1)S(1)} %get-tuple-element.289, ...), kind=kLoop, calls=%fused_computation.517 | loop fusion | flops 34304 | bytes 37121 | tf_op jit(solution)/shard_map/jit(_where)/select_n | solution.py:181
  647.8 30.1 %scatter_fusion.12 = f32[125,256]{1,0:T(8,128)S(1)} fusion(f32[125,256]{1,0:T(8,128)S(1)} %copy.935, s32[576]{0:T(1024)S(1)} %fusion.42, f32[576]{0:T(1024)S(1)} %pad_maximum_fusion.16), kind=kCustom, calls=%fused_computation.82 | custom fusion | flops 576 | bytes 11520 | tf_op jit(solution)/shard_map/scatter-add | solution.py:184
  726.2 40.0 %fusion.68 = f32[512]{0:T(512)S(1)} fusion(pred[512]{0:T(512)(128)(4,1)S(1)} %get-tuple-element.293, f32[512]{0:T(512)S(1)} %gather_fusion.29, pred[512]{0:T(512)(128)(4,1)S(1)} %get-tuple-element.291, pred[512]{0:T(512)(128)(4,1)S(1)} %get-tuple-element.290, pred[512]{0:T(512)(128)(4,1)S(1)} %get-tuple-element.289, ...), kind=kLoop, calls=%fused_computation.513 | loop fusion | flops 34304 | bytes 37121 | tf_op jit(solution)/shard_map/jit(_where)/select_n | solution.py:181
  766.2 30.1 %scatter_fusion.14 = f32[125,256]{1,0:T(8,128)S(1)} fusion(f32[125,256]{1,0:T(8,128)S(1)} %copy.942, s32[576]{0:T(1024)S(1)} %fusion.42, f32[576]{0:T(1024)S(1)} %pad_maximum_fusion.17), kind=kCustom, calls=%fused_computation.86 | custom fusion | flops 576 | bytes 11520 | tf_op jit(solution)/shard_map/scatter-add | solution.py:184
  843.8 40.0 %fusion.65 = f32[512]{0:T(512)S(1)} fusion(pred[512]{0:T(512)(128)(4,1)S(1)} %get-tuple-element.293, f32[512]{0:T(512)S(1)} %gather_fusion.34, pred[512]{0:T(512)(128)(4,1)S(1)} %get-tuple-element.291, pred[512]{0:T(512)(128)(4,1)S(1)} %get-tuple-element.290, pred[512]{0:T(512)(128)(4,1)S(1)} %get-tuple-element.289, ...), kind=kLoop, calls=%fused_computation.509 | loop fusion | flops 34304 | bytes 37121 | tf_op jit(solution)/shard_map/jit(_where)/select_n | solution.py:181
  883.8 30.1 %scatter_fusion.16 = f32[125,256]{1,0:T(8,128)S(1)} fusion(f32[125,256]{1,0:T(8,128)S(1)} %copy.949, s32[576]{0:T(1024)S(1)} %fusion.42, f32[576]{0:T(1024)S(1)} %pad_maximum_fusion.18), kind=kCustom, calls=%fused_computation.90 | custom fusion | flops 576 | bytes 11520 | tf_op jit(solution)/shard_map/scatter-add | solution.py:184
  962.1 40.0 %fusion.62 = f32[512]{0:T(512)S(1)} fusion(pred[512]{0:T(512)(128)(4,1)S(1)} %get-tuple-element.293, f32[512]{0:T(512)S(1)} %gather_fusion.39, pred[512]{0:T(512)(128)(4,1)S(1)} %get-tuple-element.291, pred[512]{0:T(512)(128)(4,1)S(1)} %get-tuple-element.290, pred[512]{0:T(512)(128)(4,1)S(1)} %get-tuple-element.289, ...), kind=kLoop, calls=%fused_computation.505 | loop fusion | flops 34304 | bytes 37121 | tf_op jit(solution)/shard_map/jit(_where)/select_n | solution.py:181
  1002.1 30.1 %scatter_fusion.18 = f32[125,256]{1,0:T(8,128)S(1)} fusion(f32[125,256]{1,0:T(8,128)S(1)} %copy.956, s32[576]{0:T(1024)S(1)} %fusion.42, f32[576]{0:T(1024)S(1)} %pad_maximum_fusion.19), kind=kCustom, calls=%fused_computation.94 | custom fusion | flops 576 | bytes 11520 | tf_op jit(solution)/shard_map/scatter-add | solution.py:184
  1079.4 40.0 %fusion.59 = f32[512]{0:T(512)S(1)} fusion(pred[512]{0:T(512)(128)(4,1)S(1)} %get-tuple-element.293, f32[512]{0:T(512)S(1)} %gather_fusion.44, pred[512]{0:T(512)(128)(4,1)S(1)} %get-tuple-element.291, pred[512]{0:T(512)(128)(4,1)S(1)} %get-tuple-element.290, pred[512]{0:T(512)(128)(4,1)S(1)} %get-tuple-element.289, ...), kind=kLoop, calls=%fused_computation.501 | loop fusion | flops 34304 | bytes 37121 | tf_op jit(solution)/shard_map/jit(_where)/select_n | solution.py:181
  1119.5 30.1 %scatter_fusion.20 = f32[125,256]{1,0:T(8,128)S(1)} fusion(f32[125,256]{1,0:T(8,128)S(1)} %copy.963, s32[576]{0:T(1024)S(1)} %fusion.42, f32[576]{0:T(1024)S(1)} %pad_maximum_fusion.20), kind=kCustom, calls=%fused_computation.98 | custom fusion | flops 576 | bytes 11520 | tf_op jit(solution)/shard_map/scatter-add | solution.py:184
  1197.9 40.0 %fusion.56 = f32[512]{0:T(512)S(1)} fusion(pred[512]{0:T(512)(128)(4,1)S(1)} %get-tuple-element.293, f32[512]{0:T(512)S(1)} %gather_fusion.49, pred[512]{0:T(512)(128)(4,1)S(1)} %get-tuple-element.291, pred[512]{0:T(512)(128)(4,1)S(1)} %get-tuple-element.290, pred[512]{0:T(512)(128)(4,1)S(1)} %get-tuple-element.289, ...), kind=kLoop, calls=%fused_computation.497 | loop fusion | flops 34304 | bytes 37121 | tf_op jit(solution)/shard_map/jit(_where)/select_n | solution.py:181
  1237.9 30.1 %scatter_fusion.22 = f32[125,256]{1,0:T(8,128)S(1)} fusion(f32[125,256]{1,0:T(8,128)S(1)} %copy.970, s32[576]{0:T(1024)S(1)} %fusion.42, f32[576]{0:T(1024)S(1)} %pad_maximum_fusion.21), kind=kCustom, calls=%fused_computation.102 | custom fusion | flops 576 | bytes 11520 | tf_op jit(solution)/shard_map/scatter-add | solution.py:184
  1306.6 5.7 all-to-all-done.11
  1315.3 39.9 %fusion.53 = f32[512]{0:T(512)S(1)} fusion(pred[512]{0:T(512)(128)(4,1)S(1)} %get-tuple-element.293, f32[512]{0:T(512)S(1)} %gather_fusion.54, pred[512]{0:T(512)(128)(4,1)S(1)} %get-tuple-element.291, pred[512]{0:T(512)(128)(4,1)S(1)} %get-tuple-element.290, pred[512]{0:T(512)(128)(4,1)S(1)} %get-tuple-element.289, ...), kind=kLoop, calls=%fused_computation.493 | loop fusion | flops 34304 | bytes 37121 | tf_op jit(solution)/shard_map/jit(_where)/select_n | solution.py:181
  1355.2 30.1 %scatter_fusion.24 = f32[125,256]{1,0:T(8,128)S(1)} fusion(f32[125,256]{1,0:T(8,128)S(1)} %copy.977, s32[576]{0:T(1024)S(1)} %fusion.42, f32[576]{0:T(1024)S(1)} %pad_maximum_fusion.22), kind=kCustom, calls=%fused_computation.106 | custom fusion | flops 576 | bytes 11520 | tf_op jit(solution)/shard_map/scatter-add | solution.py:184
  1434.0 39.9 %fusion.50 = f32[512]{0:T(512)S(1)} fusion(pred[512]{0:T(512)(128)(4,1)S(1)} %get-tuple-element.293, f32[512]{0:T(512)S(1)} %gather_fusion.59, pred[512]{0:T(512)(128)(4,1)S(1)} %get-tuple-element.291, pred[512]{0:T(512)(128)(4,1)S(1)} %get-tuple-element.290, pred[512]{0:T(512)(128)(4,1)S(1)} %get-tuple-element.289, ...), kind=kLoop, calls=%fused_computation.489 | loop fusion | flops 34304 | bytes 37121 | tf_op jit(solution)/shard_map/jit(_where)/select_n | solution.py:181
  1474.0 30.1 %scatter_fusion.26 = f32[125,256]{1,0:T(8,128)S(1)} fusion(f32[125,256]{1,0:T(8,128)S(1)} %copy.984, s32[576]{0:T(1024)S(1)} %fusion.42, f32[576]{0:T(1024)S(1)} %pad_maximum_fusion.23), kind=kCustom, calls=%fused_computation.110 | custom fusion | flops 576 | bytes 11520 | tf_op jit(solution)/shard_map/scatter-add | solution.py:184
  (830 shorter events, 562.2 us)
Async XLA Ops:
  7.8 7.6 collective-permute-start
  8.3 7.1 collective-permute-start.3
  93.6 13.0 all-to-all-start
  120.4 12.6 all-to-all-start.1
  210.0 4.6 collective-permute-start.8
  225.4 6.0 collective-permute-start.9
  240.1 11.3 all-to-all-start.2
  328.5 4.6 collective-permute-start.13
  343.9 5.0 collective-permute-start.14
  357.5 11.5 all-to-all-start.3
  446.1 4.6 collective-permute-start.18
  461.5 6.0 collective-permute-start.19
  476.1 11.2 all-to-all-start.4
  564.5 4.6 collective-permute-start.23
  579.8 5.0 collective-permute-start.24
  593.5 11.3 all-to-all-start.5
  681.8 4.6 collective-permute-start.28
  697.1 6.0 collective-permute-start.29
  711.8 11.3 all-to-all-start.6
  815.5 5.0 collective-permute-start.34
  829.2 11.5 all-to-all-start.7
  933.1 6.1 collective-permute-start.39
  947.8 11.2 all-to-all-start.8
  1051.4 5.0 collective-permute-start.44
  1065.1 11.3 all-to-all-start.9
  1168.9 6.0 collective-permute-start.49
  1183.5 11.3 all-to-all-start.10
  1271.9 4.6 collective-permute-start.53
  1287.3 5.0 collective-permute-start.54
  1300.9 11.3 all-to-all-start.11
  1404.5 6.8 collective-permute-start.59
  1420.0 11.0 all-to-all-start.12
  (50 other events, 222.3 us)
